TPU v7x, 32 devices: a whole 2x2x4 slice. The times are simulated.
32 devices in a mesh: row: 4 (over z), col: 4 (over x, core), grp: 2 (over y).
Axes of the slice: x: 2, y: 2, z: 4, core: 2. Of those that a mesh axis runs over, the one named last changes fastest.
Arguments:
- matrix: float32 [16384, 16384], P('row', ('col', 'grp')), may hold values from -8 to 8, as said below
- basis_rows: float32 [4096, 16384], P(('col', 'grp'), 'row'), may hold values from -6 to 6
- reflectors: float32 [16384, 512], P('row'), may hold values from -0.125 to 0.125
- tfactor: float32 [512, 512], replicated, may hold values from -0.25 to 2, as said below
Outputs:
- new_matrix: float32 [16384, 16384], P('row', ('col', 'grp'))
- new_basis: float32 [4096, 16384], P(('col', 'grp'), 'row')
Inputs may be any that keep to these rules, and one draw needn't show every extreme that they name: The matrix A that it represents is symmetric. `tfactor`: upper triangular: zero below the diagonal, diagonal between 1 and 2.
All inputs are finite; a program needn't handle non-finite values.
Results may differ from a plain program's by a relative error of at most 0.000073.
Values sent between devices are 32-bit elements; how exact they have to be, the bound alone decides.
A program may use at most 192 MiB of HBM per device.

v0:
```python
import jax
import jax.numpy as jnp
from jax import lax
from jax.sharding import PartitionSpec as P


def on_device(matrix, basis_rows, reflectors, tfactor):
    highest = lax.Precision.HIGHEST
    groups = lax.axis_size(("col", "grp"))
    member = lax.axis_index(("col", "grp"))
    slice_rows = reflectors.shape[0] // groups
    own_v = lax.dynamic_slice_in_dim(reflectors, member * slice_rows, slice_rows, 0)
    v_col = lax.all_gather(own_v, "row", axis=0, tiled=True)
    applied = lax.psum_scatter(
        jnp.dot(matrix, v_col, precision=highest, preferred_element_type=jnp.float32),
        ("col", "grp"),
        scatter_dimension=0,
        tiled=True,
    )
    w_slice = jnp.dot(applied, tfactor, precision=highest, preferred_element_type=jnp.float32)
    cross = lax.psum(
        jnp.dot(own_v.T, w_slice, precision=highest, preferred_element_type=jnp.float32),
        ("row", "col", "grp"),
    )
    inner = jnp.dot(tfactor.T, cross, precision=highest, preferred_element_type=jnp.float32)
    z_slice = w_slice - 0.5 * jnp.dot(
        own_v, inner, precision=highest, preferred_element_type=jnp.float32
    )
    z_row = lax.all_gather(z_slice, ("col", "grp"), axis=0, tiled=True)
    z_col = lax.all_gather(z_slice, "row", axis=0, tiled=True)
    new_matrix = matrix - jnp.dot(
        reflectors, z_col.T, precision=highest, preferred_element_type=jnp.float32
    )
    new_matrix = new_matrix - jnp.dot(
        z_row, v_col.T, precision=highest, preferred_element_type=jnp.float32
    )
    q_proj = lax.psum(
        jnp.dot(basis_rows, reflectors, precision=highest, preferred_element_type=jnp.float32),
        "row",
    )
    q_fact = jnp.dot(q_proj, tfactor, precision=highest, preferred_element_type=jnp.float32)
    new_basis = basis_rows - jnp.dot(
        q_fact, reflectors.T, precision=highest, preferred_element_type=jnp.float32
    )
    return (new_matrix, new_basis)


def solution(mesh):
    placed = (P("row", ("col", "grp")), P(("col", "grp"), "row"), P("row", None), P())
    return jax.shard_map(
        on_device,
        mesh=mesh,
        in_specs=placed,
        out_specs=(P("row", ("col", "grp")), P(("col", "grp"), "row")),
        check_vma=False,
    )
```

profile of v0, /device:TPU:0, one launch (start us, length us, event | category | flops | bytes accessed | tf_op | source)
XLA Modules:
  0.0 707.9 jit_solution(3605354515648667149)
XLA Ops:
  7.2 0.0 copy-start
  7.2 0.0 all-gather.4.cloned.1.call-start
  7.2 2.3 constant_dynamic-slice_fusion
  9.6 0.0 all-gather.4.cloned.1.call-update
  9.6 0.0 reduce-scatter.2.cloned.1.call-start
  9.7 84.0 %all-gather.4.cloned.1.call-done = f32[2048,512]{1,0:T(8,128)} async-done(((f32[512,512]{1,0:T(8,128)}), f32[2048,512]{1,0:T(8,128)}) %all-gather.4.cloned.1.call-update) | async-done | bytes 4194320 | tf_op jit(solution)/shard_map/all_gather | solution.py:13
  93.6 111.4 %convolution_bitcast_fusion = f32[4096,512]{0,1:T(8,128)} fusion(f32[2048,512]{1,0:T(8,128)} %all-gather.4.cloned.1.call-done, f32[4096,2048]{1,0:T(8,128)} %param.4), kind=kOutput, calls=%fused_computation.2 | convolution fusion | flops 51539607552 | bytes 46137344 | tf_op jit(solution)/shard_map/dot_general | solution.py:15
  205.1 0.0 copy-start.2
  205.1 0.0 reduce-scatter.2.cloned.1.call-update
  205.1 0.0 all-reduce.3.cloned.1.call-start
  205.1 69.9 %reduce-scatter.2.cloned.1.call-done = f32[512,512]{0,1:T(8,128)} async-done(((f32[4096,512]{0,1:T(8,128)}), f32[512,512]{0,1:T(8,128)}) %reduce-scatter.2.cloned.1.call-update) | async-done | bytes 1048592 | tf_op jit(solution)/shard_map/reduce_scatter | solution.py:14
  275.1 0.0 copy-done
  275.1 3.1 fusion.2
  278.2 0.0 copy-done.2
  278.2 2.8 fusion.3
  281.0 0.0 all-reduce.3.cloned.1.call-update
  281.0 0.0 all-reduce.5.cloned.1.call-start
  281.1 17.3 %fusion.6 = f32[512,512]{1,0:T(8,128)} fusion(f32[512,4096]{1,0:T(8,128)} %param.5, f32[4096,512]{1,0:T(8,128)} %param.6), kind=kOutput, calls=%fused_computation.11 | convolution fusion | flops 12884901888 | bytes 17825792 | tf_op jit(solution)/shard_map/dot_general | solution.py:38
  298.4 0.0 all-reduce.5.cloned.1.call-update
  298.4 0.0 all-gather.8.cloned.1.call-start
  298.4 113.4 %all-reduce.3.cloned.1.call-done = f32[512,512]{1,0:T(8,128)} async-done(((f32[512,512]{1,0:T(8,128)}), f32[512,512]{1,0:T(8,128)}) %all-reduce.3.cloned.1.call-update) | async-done | bytes 1048592 | tf_op jit(solution)/shard_map/psum | solution.py:21
  411.9 3.1 fusion.4
  414.9 2.9 fusion.1
  417.8 0.0 all-gather.8.cloned.1.call-update
  417.8 0.0 all-gather.6.cloned.1.call-start
  417.9 0.5 all-gather.6.cloned.1.call-update
  418.4 31.6 %copy.6 = f32[4096,2048]{0,1:T(8,128)} copy(f32[4096,2048]{1,0:T(8,128)} %param.4) | data formatting | bytes 67108864 | tf_op args[0]
  450.0 15.5 %all-reduce.5.cloned.1.call-done = f32[512,512]{1,0:T(8,128)} async-done(((f32[512,512]{1,0:T(8,128)}), f32[512,512]{1,0:T(8,128)}) %all-reduce.5.cloned.1.call-update) | async-done | bytes 1048592 | tf_op jit(solution)/shard_map/psum | solution.py:37
  465.5 3.1 fusion.7
  468.6 19.2 %convolution_subtract_fusion = f32[512,4096]{1,0:T(8,128)} fusion(f32[512,4096]{1,0:T(8,128)} %param.5, f32[512,512]{1,0:T(8,128)S(1)} %fusion.7, f32[4096,512]{1,0:T(8,128)} %param.6), kind=kOutput, calls=%fused_computation.3 | convolution fusion | flops 12886999040 | bytes 26214400 | tf_op jit(solution)/shard_map/dot_general | solution.py:42
  487.8 33.0 %all-gather.8.cloned.1.call-done = f32[4096,512]{1,0:T(8,128)} async-done(((f32[512,512]{1,0:T(8,128)}), f32[4096,512]{1,0:T(8,128)}) %all-gather.8.cloned.1.call-update) | async-done | bytes 8388624 | tf_op jit(solution)/shard_map/all_gather | solution.py:29
  520.8 59.0 %fusion.5 = f32[4096,2048]{0,1:T(8,128)} fusion(f32[4096,512]{1,0:T(8,128)} %all-gather.8.cloned.1.call-done, f32[2048,512]{1,0:T(8,128)} %all-gather.4.cloned.1.call-done), kind=kOutput, calls=%fused_computation.10 | convolution fusion | flops 51539607552 | bytes 46137344 | tf_op jit(solution)/shard_map/dot_general | solution.py:34
  579.8 23.2 %all-gather.6.cloned.1.call-done = f32[2048,512]{1,0:T(8,128)} async-done(((f32[512,512]{1,0:T(8,128)}), f32[2048,512]{1,0:T(8,128)}) %all-gather.6.cloned.1.call-update) | async-done | bytes 4194320 | tf_op jit(solution)/shard_map/all_gather | solution.py:30
  603.0 64.4 %fusion = f32[4096,2048]{0,1:T(8,128)} fusion(f32[4096,2048]{0,1:T(8,128)} %fusion.5, f32[4096,2048]{0,1:T(8,128)} %copy.6, f32[2048,512]{1,0:T(8,128)} %all-gather.6.cloned.1.call-done, f32[4096,512]{1,0:T(8,128)} %param.6), kind=kOutput, calls=%fused_computation.1 | convolution fusion | flops 51556384768 | bytes 113246208 | tf_op jit(solution)/shard_map/dot_general | solution.py:31
  667.4 0.0 copy-start.1
  667.4 33.4 %copy.8 = f32[4096,2048]{1,0:T(8,128)} copy(f32[4096,2048]{0,1:T(8,128)} %fusion) | data formatting | bytes 67108864
  700.8 0.0 copy-done.1
Async XLA Ops:
  7.2 267.9 %copy-start = (f32[512,512]{1,0:T(8,128)S(1)}, f32[512,512]{1,0:T(8,128)}, u32[]{:S(2)}) copy-start(f32[512,512]{1,0:T(8,128)} %param.7) | copy-start | bytes 3145732
  7.2 86.4 %all-gather.4.cloned.1.call-start = ((), (), s32[]{:S(2)}) async-start(), calls=%async_computation.1 | async-start | bytes 5242880 | tf_op jit(solution)/shard_map/all_gather | solution.py:13
  9.6 265.5 %reduce-scatter.2.cloned.1.call-start = ((), (), s32[]{:S(2)}) async-start(), calls=%async_computation.2 | async-start | bytes 9437184 | tf_op jit(solution)/shard_map/reduce_scatter | solution.py:14
  205.1 73.1 %copy-start.2 = (f32[512,512]{1,0:T(8,128)S(1)}, f32[512,512]{1,0:T(8,128)}, u32[]{:S(2)}) copy-start(f32[512,512]{1,0:T(8,128)} %constant_dynamic-slice_fusion) | copy-start | bytes 3145732
  205.1 206.8 %all-reduce.3.cloned.1.call-start = ((), (), s32[]{:S(2)}) async-start(), calls=%async_computation.3 | async-start | bytes 2097152 | tf_op jit(solution)/shard_map/psum | solution.py:21
  281.0 184.5 %all-reduce.5.cloned.1.call-start = ((), (), s32[]{:S(2)}) async-start(), calls=%async_computation.6 | async-start | bytes 2097152 | tf_op jit(solution)/shard_map/psum | solution.py:37
  298.4 222.4 %all-gather.8.cloned.1.call-start = ((), (), s32[]{:S(2)}) async-start(), calls=%async_computation.5 | async-start | bytes 9437184 | tf_op jit(solution)/shard_map/all_gather | solution.py:29
  417.8 185.2 %all-gather.6.cloned.1.call-start = ((), (), s32[]{:S(2)}) async-start(), calls=%async_computation.4 | async-start | bytes 5242880 | tf_op jit(solution)/shard_map/all_gather | solution.py:30
  667.4 33.4 %copy-start.1 = (f32[512,512]{1,0:T(8,128)S(1)}, f32[512,512]{1,0:T(8,128)}, u32[]{:S(2)}) copy-start(f32[512,512]{1,0:T(8,128)} %param.7) | copy-start | bytes 3145732
Sparse Core Ops, SparseCore 0:
  10.1 83.4 all-gather.3
  205.2 69.8 reduce-scatter.1
  281.1 130.6 all-reduce.2
  414.7 50.8 all-reduce.4
  467.3 53.5 all-gather.7
  522.2 80.7 all-gather.5
where the time goes:
time: 718 us; the launch traced here: 708 us
  waiting for transfers between devices  340 us (47%)
  matrix products  286 us (40%)
  local copies, waits for them, and re-layouts  67.4 us (9%)
  between operations  14.4 us (2%)
    psum x1, waiting for transfers between devices, on_device(): lax.psum(jnp.dot(own_v.T, w_slice, precision=highest, preferred_element_t...  113 us
    dot_general x1, matrix products, on_device(): jnp.dot(matrix, v_col, precision=highest, preferred_element_type=jnp.floa...  111 us
    all_gather x1, waiting for transfers between devices, on_device(): v_col = lax.all_gather(own_v, 'row', axis=0, tiled=True)  84 us
    reduce_scatter x1, waiting for transfers between devices, on_device(): lax.psum_scatter(jnp.dot(matrix, v_col, precision=highest, preferred_elem...  69.9 us
    unnamed x8, local copies, waits for them, and re-layouts  65.1 us
    dot_general x1, matrix products, on_device(): jnp.dot(reflectors, z_col.T, precision=highest, preferred_element_type=jn...  64.4 us
    dot_general x1, matrix products, on_device(): jnp.dot(z_row, v_col.T, precision=highest, preferred_element_type=jnp.flo...  59 us
    all_gather x1, waiting for transfers between devices, on_device(): z_row = lax.all_gather(z_slice, ('col', 'grp'), axis=0, tiled=True)  33 us
  transfers between devices with their start and end apart: 6, of which 6 were waited for; matrix products, arithmetic and copies ran while one was open for 19% of the time, Pallas kernels for 0%

commit v1 on v0

v1 whole, which is shorter than its diff:
```python
import jax
import jax.numpy as jnp
from jax import lax
from jax.experimental import pallas as pl
from jax.experimental.pallas import tpu as pltpu
from jax.sharding import PartitionSpec as P


def halves(x):
    high = x.astype(jnp.bfloat16)
    return high, (x - high.astype(jnp.float32)).astype(jnp.bfloat16)


def apply_kernel(index_ref, a_ref, v_ref, *rest):
    out_ref = rest[-1]
    a_high, a_low = halves(a_ref[...])
    v_high, v_low = halves(v_ref[...])
    product = jnp.dot(
        jnp.concatenate([a_high, a_low, a_high], axis=1),
        jnp.concatenate([v_high, v_high, v_low], axis=0),
        preferred_element_type=jnp.float32,
    )
    out_ref[...] = product if len(rest) == 1 else rest[0][...] + product


def apply_chunk(matrix, chunk, total, index):
    rows, (depth, wide) = matrix.shape[0], chunk.shape
    tile = min(512, rows)
    specs = [
        pl.BlockSpec((tile, depth), lambda i, c: (i, c[0])),
        pl.BlockSpec((depth, wide), lambda i, c: (0, 0)),
    ]
    args = [matrix, chunk]
    if total is not None:
        specs.append(pl.BlockSpec((tile, wide), lambda i, c: (i, 0)))
        args.append(total)
    return pl.pallas_call(
        apply_kernel,
        out_shape=jax.ShapeDtypeStruct((rows, wide), jnp.float32),
        grid_spec=pltpu.PrefetchScalarGridSpec(
            num_scalar_prefetch=1,
            grid=(rows // tile,),
            in_specs=specs,
            out_specs=pl.BlockSpec((tile, wide), lambda i, c: (i, 0)),
        ),
        cost_estimate=pl.CostEstimate(
            flops=6 * rows * depth * wide,
            bytes_accessed=4 * rows * (depth + 2 * wide),
            transcendentals=0,
        ),
        name="apply_chunk",
    )(index, *args)


def update_kernel(order_ref, a_ref, near_ref, far_ref, vr_ref, vc_ref, zc_ref, *rest):
    out_ref, right = rest[-2:]

    @pl.when(pl.program_id(0) == 0)
    def _():
        v_high, v_low = halves(vc_ref[...])
        z_high, z_low = halves(zc_ref[...])
        right[...] = jnp.concatenate([v_high, v_high, v_low, z_high, z_high, z_low], axis=1)

    first = pl.program_id(0) < pl.num_programs(0) // 2
    w_high, w_low = halves(jnp.where(first, near_ref[...], far_ref[...]))
    v_high, v_low = halves(vr_ref[...])
    left = jnp.concatenate([w_high, w_low, w_high, v_high, v_low, v_high], axis=1)
    out_ref[...] = a_ref[...] - lax.dot_general(
        left, right[...], (((1,), (1,)), ((), ())), preferred_element_type=jnp.float32
    )


def update_chunk(matrix, w_near, w_far, v_row, v_chunk, z_chunk, order, out):
    rows, (depth, wide) = matrix.shape[0], v_chunk.shape
    steps = order.shape[0] - 1
    tile, half = rows // steps, steps // 2
    specs = [
        pl.BlockSpec((tile, depth), lambda i, c: (c[i + 1], c[0])),
        pl.BlockSpec((tile, wide), lambda i, c: (jnp.minimum(i, half - 1), 0)),
        pl.BlockSpec((tile, wide), lambda i, c: (jnp.maximum(i - half, 0), 0)),
        pl.BlockSpec((tile, wide), lambda i, c: (c[i + 1], 0)),
        pl.BlockSpec((depth, wide), lambda i, c: (0, 0)),
        pl.BlockSpec((depth, wide), lambda i, c: (0, 0)),
    ]
    args = [matrix, w_near, w_far, v_row, v_chunk, z_chunk]
    alias = {}
    if out is not None:
        specs.append(pl.BlockSpec(memory_space=pl.ANY))
        args.append(out)
        alias = {7: 0}
    return pl.pallas_call(
        update_kernel,
        out_shape=jax.ShapeDtypeStruct(matrix.shape, jnp.float32),
        grid_spec=pltpu.PrefetchScalarGridSpec(
            num_scalar_prefetch=1,
            grid=(steps,),
            in_specs=specs,
            out_specs=pl.BlockSpec((tile, depth), lambda i, c: (c[i + 1], c[0])),
            scratch_shapes=[pltpu.VMEM((depth, 6 * wide), jnp.bfloat16)],
        ),
        input_output_aliases=alias,
        cost_estimate=pl.CostEstimate(
            flops=12 * rows * depth * wide,
            bytes_accessed=8 * rows * (depth + wide),
            transcendentals=0,
        ),
        name="update_chunk",
    )(order, *args)


def dot(a, b):
    return jnp.dot(a, b, precision=lax.Precision.HIGH, preferred_element_type=jnp.float32)


def swap(x, axis, bit):
    count = lax.axis_size(axis)
    return lax.ppermute(x, axis, [(i, i ^ bit) for i in range(count)])


def pick(x, index, axis):
    return lax.dynamic_index_in_dim(x, index, axis, keepdims=False)


def scatter_sum(total):
    if lax.axis_size("col") != 4 or lax.axis_size("grp") != 2:
        return lax.psum_scatter(total, ("col", "grp"), scatter_dimension=0, tiled=True)
    col, y = lax.axis_index("col"), lax.axis_index("grp")
    x, core = col // 2, col % 2
    depth, wide = total.shape[0] // 8, total.shape[1]
    total = total.reshape(2, 2, 2, depth, wide)
    mine = pick(total, core, 1) + swap(pick(total, 1 - core, 1), "col", 1)
    near, far = mine[:, :, : depth // 2], mine[:, :, depth // 2 :]
    near_in = swap(pick(near, 1 - x, 0), "col", 2)
    far_in = swap(pick(far, 1 - y, 1), "grp", 1)
    near = pick(near, x, 0) + near_in
    far = pick(far, y, 1) + far_in
    near_in = swap(pick(near, 1 - y, 0), "grp", 1)
    far_in = swap(pick(far, 1 - x, 0), "col", 2)
    return jnp.concatenate([pick(near, y, 0) + near_in, pick(far, x, 0) + far_in], axis=0)


def gather_rows(own):
    if lax.axis_size("col") != 4 or lax.axis_size("grp") != 2:
        whole = lax.all_gather(own, ("col", "grp"), axis=0, tiled=True)
        half = whole.shape[0] // 2
        tiles = jnp.arange(whole.shape[0] // own.shape[0])
        return whole[:half], whole[half:], tiles
    depth, _ = own.shape
    near, far = own[None, : depth // 2], own[None, depth // 2 :]
    near = jnp.concatenate([near, swap(near, "grp", 1)])
    far = jnp.concatenate([far, swap(far, "col", 2)])
    near_in, far_in = swap(near, "col", 2), swap(far, "grp", 1)
    near = jnp.concatenate([near, near_in])
    tiles = []
    for tile in range(4):
        source, place = (far, far_in)[tile % 2], tile // 2
        tiles += [near[tile], source[place]]
    mine = jnp.concatenate(tiles, axis=0)
    col, y = lax.axis_index("col"), lax.axis_index("grp")
    bits = jnp.arange(8)
    cols = col ^ (2 * (bits // 2 % 2) + bits // 4)
    rest = swap(mine, "col", 1)
    return mine, rest, cols * 2 + (y ^ (bits % 2))


def step(matrix, basis_rows, reflectors, tfactor):
    plane = ("col", "grp")
    member, groups = lax.axis_index(plane), lax.axis_size(plane)
    row, count = lax.axis_index("row"), lax.axis_size("row")
    ring = [(i, (i + 1) % count) for i in range(count)]
    slice_rows = reflectors.shape[0] // groups
    own_v = lax.dynamic_slice_in_dim(reflectors, member * slice_rows, slice_rows, 0)

    v_chunks, owners = [own_v], []
    for step in range(count):
        owners.append(((row - step + count) % count).astype(jnp.int32).reshape(1))
        if step + 1 < count:
            v_chunks.append(lax.ppermute(v_chunks[-1], "row", ring))
    total = apply_chunk(matrix, own_v, None, owners[0])
    total, q_proj = lax.optimization_barrier((total, dot(basis_rows, reflectors)))
    q_proj = lax.psum(q_proj, "row")
    for chunk, owner in zip(v_chunks[1:], owners[1:]):
        total = apply_chunk(matrix, chunk, total, owner)

    cross, total = lax.optimization_barrier((dot(reflectors.T, total), total))
    cross = lax.psum_scatter(cross, plane, scatter_dimension=0, tiled=True)
    applied = scatter_sum(total)
    w_slice = dot(applied, tfactor)
    cross, w_slice = lax.optimization_barrier((cross, w_slice))
    cross = lax.all_gather(lax.psum(cross, "row"), plane, axis=0, tiled=True)
    w_chunks = [w_slice]
    for _ in range(count - 1):
        w_chunks.append(lax.ppermute(w_chunks[-1], "row", ring))
    w_near, w_far, tiles = gather_rows(w_slice)
    inner = dot(tfactor.T, dot(cross, tfactor))

    out = None
    for v_chunk, w_chunk, owner in zip(v_chunks, w_chunks, owners):
        if out is not None:
            out, w_chunk = lax.optimization_barrier((out, w_chunk))
        z_chunk = w_chunk - dot(v_chunk, inner.T)
        order = jnp.concatenate([owner, tiles.astype(jnp.int32)])
        out = update_chunk(matrix, w_near, w_far, reflectors, v_chunk, z_chunk, order, out)

    new_basis = basis_rows - dot(dot(q_proj, tfactor), reflectors.T)
    return (out, new_basis)


def solution(mesh):
    placed = (P("row", ("col", "grp")), P(("col", "grp"), "row"), P("row", None), P())
    return jax.shard_map(
        step,
        mesh=mesh,
        in_specs=placed,
        out_specs=(P("row", ("col", "grp")), P(("col", "grp"), "row")),
        check_vma=False,
    )
```

time: 718 us -> 435 us (0.61)
  matrix products: 286 us -> 60.5 us
  waiting for transfers between devices: 340 us -> 142 us
  Pallas kernels: 0 us -> 140 us
  local copies, waits for them, and re-layouts: 67.4 us -> 27 us
  starting transfers between devices: 0.25 us -> 25.1 us
  other arithmetic: 0 us -> 20.2 us
    dot_general x10 -> x11, matrix products: 286 us -> 60.5 us  [dot(): jnp.dot(a, b, precision=lax.Precision.HIGH, preferred_element_type=jnp.fl...]
    pallas_call x0 -> x8, Pallas kernels: none -> 140 us  [the longest x4 85.1 us: update_chunk(): pl.pallas_call(update_kernel, out_shape=jax.ShapeDtypeStruct(matrix.shape...]
    all_gather x3 -> x1, waiting for transfers between devices: 140 us -> 0.01 us  [step(): cross = lax.all_gather(lax.psum(cross, 'row'), plane, axis=0, tiled=True)]
    ppermute x0 -> x16, waiting for transfers between devices: none -> 84.6 us  [the longest x10 47.9 us: swap(): return lax.ppermute(x, axis, [(i, i ^ bit) for i in range(count)])]
    psum x2 -> x1, waiting for transfers between devices: 129 us -> 47.4 us  [step(): cross = lax.all_gather(lax.psum(cross, 'row'), plane, axis=0, tiled=True)]
    reduce_scatter x1 -> x0, waiting for transfers between devices: 69.9 us -> none  [on_device(): lax.psum_scatter(jnp.dot(matrix, v_col, precision=highest, preferred_elem...]
    unnamed x8 -> x35, local copies, waits for them, and re-layouts: 65.1 us -> 14.3 us
    ppermute x0 -> x16, starting transfers between devices: none -> 15.2 us  [the longest x10 10.2 us: swap(): return lax.ppermute(x, axis, [(i, i ^ bit) for i in range(count)])]
  transfers between devices with their start and end apart: 6 -> 19, of which waited for: 6 -> 10; matrix products, arithmetic and copies ran while one was open for 19% -> 17% of each run, Pallas kernels for 0% -> 24%
where the time goes in v1:
time: 435 us; the launch traced here: 429 us
  waiting for transfers between devices  142 us (33%)
  Pallas kernels  140 us (32%)
  matrix products  60.5 us (14%)
  local copies, waits for them, and re-layouts  27 us (6%)
  starting transfers between devices  25.1 us (6%)
  other arithmetic  20.2 us (5%)
  between operations  14.2 us (3%)
    pallas_call x4, Pallas kernels, update_chunk(): pl.pallas_call(update_kernel, out_shape=jax.ShapeDtypeStruct(matrix.shape...  85.1 us
    dot_general x11, matrix products, dot(): jnp.dot(a, b, precision=lax.Precision.HIGH, preferred_element_type=jnp.fl...  60.5 us
    pallas_call x4, Pallas kernels, apply_chunk(): pl.pallas_call(apply_kernel, out_shape=jax.ShapeDtypeStruct((rows, wide),...  55.2 us
    ppermute x10, waiting for transfers between devices, swap(): return lax.ppermute(x, axis, [(i, i ^ bit) for i in range(count)])  47.9 us
    psum x1, waiting for transfers between devices, step(): cross = lax.all_gather(lax.psum(cross, 'row'), plane, axis=0, tiled=True)  47.4 us
    ppermute x3, waiting for transfers between devices, step(): v_chunks.append(lax.ppermute(v_chunks[-1], 'row', ring))  26 us
    unnamed x35, local copies, waits for them, and re-layouts  14.3 us
    ppermute x3, waiting for transfers between devices, step(): w_chunks.append(lax.ppermute(w_chunks[-1], 'row', ring))  10.7 us
  transfers between devices with their start and end apart: 19, of which 10 were waited for; matrix products, arithmetic and copies ran while one was open for 17% of the time, Pallas kernels for 24%

profile of v1, /device:TPU:0, one launch (start us, length us, event | category | flops | bytes accessed | tf_op | source)
XLA Modules:
  0.0 429.3 jit_solution(3065523883513019266)
XLA Ops:
  7.2 1.4 constant_dynamic-slice_fusion.v_ref.vc_ref
  8.6 3.1 collective-permute-start
  11.7 25.2 %collective-permute-done.v_ref.vc_ref = f32[512,512]{1,0:T(8,128)S(1)} collective-permute-done((f32[512,512]{1,0:T(8,128)S(1)}, f32[512,512]{1,0:T(8,128)S(1)}, u32[]{:S(2)}, u32[]{:S(2)}) %collective-permute-start) | collective-permute-done | bytes 1048608 | tf_op jit(solution)/shard_map/ppermute | solution.py:178
  36.9 12.9 %apply_chunk.4.rest_0_ = f32[4096,512]{1,0:T(8,128)} custom-call(s32[1]{0:T(128)} %bitcast.3.index_ref, f32[4096,2048]{1,0:T(8,128)} %a_ref.15, f32[512,512]{1,0:T(8,128)} %copy-done.3), custom_call_target="tpu_custom_call" | custom-call | flops 6442450944 | bytes 25165824 | tf_op jit(solution)/shard_map/apply_chunk/pallas_call | solution.py:37
  49.9 12.5 %fusion.17 = f32[512,512]{1,0:T(8,128)} fusion(f32[512,4096]{1,0:T(8,128)} %param.5, f32[4096,512]{1,0:T(8,128)} %vr_ref.7), kind=kOutput, calls=%fused_computation.57 | convolution fusion | flops 6442450944 | bytes 17825792 | tf_op jit(solution)/shard_map/dot_general | solution.py:112
  63.6 14.1 %apply_chunk.5.rest_0_ = f32[4096,512]{1,0:T(8,128)} custom-call(s32[1]{0:T(128)} %bitcast.2.index_ref, f32[4096,2048]{1,0:T(8,128)} %a_ref.15, f32[512,512]{1,0:T(8,128)} %copy-done.5, f32[4096,512]{1,0:T(8,128)} %apply_chunk.4.rest_0_), custom_call_target="tpu_custom_call" | custom-call | flops 6442450944 | bytes 25165824 | tf_op jit(solution)/shard_map/apply_chunk/pallas_call | solution.py:37
  77.7 14.1 %apply_chunk.6.rest_0_ = f32[4096,512]{1,0:T(8,128)} custom-call(s32[1]{0:T(128)} %bitcast.1.index_ref, f32[4096,2048]{1,0:T(8,128)} %a_ref.15, f32[512,512]{1,0:T(8,128)} %collective-permute-done.1.v_ref.vc_ref, f32[4096,512]{1,0:T(8,128)} %apply_chunk.5.rest_0_), custom_call_target="tpu_custom_call" | custom-call | flops 6442450944 | bytes 25165824 | tf_op jit(solution)/shard_map/apply_chunk/pallas_call | solution.py:37
  91.8 1.0 copy-done.7
  92.8 14.1 %apply_chunk.7 = f32[4096,512]{1,0:T(8,128)} custom-call(s32[1]{0:T(128)} %bitcast.index_ref, f32[4096,2048]{1,0:T(8,128)} %a_ref.15, f32[512,512]{1,0:T(8,128)} %copy-done.7, f32[4096,512]{1,0:T(8,128)} %apply_chunk.6.rest_0_), custom_call_target="tpu_custom_call" | custom-call | flops 6442450944 | bytes 25165824 | tf_op jit(solution)/shard_map/apply_chunk/pallas_call | solution.py:37
  106.9 19.2 %convolution_bitcast_fusion = f32[512,512]{0,1:T(8,128)} fusion(f32[4096,512]{1,0:T(8,128)} %apply_chunk.7, f32[4096,512]{1,0:T(8,128)} %vr_ref.7), kind=kOutput, calls=%fused_computation.4 | convolution fusion | flops 6442450944 | bytes 17825792 | tf_op jit(solution)/shard_map/dot_general | solution.py:112
  126.0 2.5 dynamic-slice_bitcast_fusion
  128.5 7.5 %collective-permute-done.3 = f32[2,2,512,512]{3,2,1,0:T(8,128)} collective-permute-done((f32[2,2,512,512]{3,2,1,0:T(8,128)}, f32[2,2,512,512]{3,2,1,0:T(8,128)}, u32[]{:S(2)}, u32[]{:S(2)}) %collective-permute-start.3) | collective-permute-done | bytes 4194336 | tf_op jit(solution)/shard_map/ppermute | solution.py:117
  136.0 4.5 %bitcast_add_fusion = f32[2,2,512,512]{3,2,1,0:T(8,128)S(1)} fusion(f32[2,2,512,512]{3,2,1,0:T(8,128)} %collective-permute-done.3, f32[2,2,2,512,512]{4,3,2,1,0:T(8,128)} %bitcast.73, s32[]{:T(128)S(6)} %select_n.84), kind=kLoop, calls=%fused_computation.1 | loop fusion | flops 1048576 | bytes 12582916 | tf_op jit(solution)/shard_map/add | solution.py:131
  140.9 1.3 copy-done.9
  142.2 1.0 dynamic-slice_bitcast_fusion.1
  143.3 1.5 collective-permute-start.6
  144.8 1.0 dynamic-slice_bitcast_fusion.2
  145.8 1.5 collective-permute-start.4
  147.3 2.5 copy.10
  149.9 9.8 %all-reduce.3.cloned.1.call-start = ((), (), s32[]{:S(2)}) async-start(), calls=%async_computation.3 | async-start | bytes 2621440 | tf_op jit(solution)/shard_map/psum | solution.py:190
  159.7 9.1 %collective-permute-done.6 = f32[2,256,512]{2,1,0:T(8,128)} collective-permute-done((f32[2,256,512]{2,1,0:T(8,128)}, f32[2,256,512]{2,1,0:T(8,128)}, u32[]{:S(2)}, u32[]{:S(2)}) %collective-permute-start.6) | collective-permute-done | bytes 1048608 | tf_op jit(solution)/shard_map/ppermute | solution.py:117
  168.8 1.9 bitcast_add_fusion.1
  170.7 0.9 dynamic-slice_bitcast_fusion.3
  171.6 1.5 collective-permute-start.7
  173.1 1.4 bitcast_add_fusion.2
  174.7 0.9 copy-done.13
  175.6 1.5 collective-permute-start.5
  177.1 10.0 %reduce-scatter.4.cloned.1.call-done = f32[64,512]{1,0:T(8,128)} async-done(((f32[512,512]{1,0:T(8,128)}), f32[64,512]{1,0:T(8,128)}) %reduce-scatter.4.cloned.1.call-update) | async-done | bytes 131088
  187.1 1.7 copy.11
  188.8 1.3 bitcast_add_fusion.3
  190.1 1.1 bitcast_add_fusion.4
  191.3 1.0 fusion
  192.4 1.6 collective-permute-start.9
  194.5 11.7 %collective-permute-done.9 = f32[1,256,512]{2,1,0:T(8,128)S(1)} collective-permute-done((f32[1,256,512]{2,1,0:T(8,128)S(1)}, f32[1,256,512]{2,1,0:T(8,128)S(1)}, u32[]{:S(2)}, u32[]{:S(2)}) %collective-permute-start.9) | collective-permute-done | bytes 524320 | tf_op jit(solution)/shard_map/ppermute | solution.py:117
  206.1 1.0 pad_maximum_fusion
  207.2 1.4 collective-permute-start.10
  208.6 1.0 pad_maximum_fusion.1
  210.3 1.1 constant_dynamic-update-slice_fusion
  211.4 0.8 bitcast_dynamic-update-slice_fusion.1
  212.2 19.3 %collective-permute-done.10 = f32[2,256,512]{2,1,0:T(8,128)} collective-permute-done((f32[2,256,512]{2,1,0:T(8,128)}, f32[2,256,512]{2,1,0:T(8,128)}, u32[]{:S(2)}, u32[]{:S(2)}) %collective-permute-start.10) | collective-permute-done | bytes 1048608 | tf_op jit(solution)/shard_map/ppermute | solution.py:117
  231.5 1.9 fusion.7
  233.7 1.9 fusion.6
  235.6 0.8 bitcast_dynamic-update-slice_fusion
  236.4 1.9 fusion.5
  238.3 1.9 fusion.4.near_ref
  240.3 1.5 collective-permute-start.13
  241.7 47.4 %all-reduce.3.cloned.1.call-done = (f32[64,512]{0,1:T(8,128)}, f32[512,512]{1,0:T(8,128)}) async-done(((f32[64,512]{0,1:T(8,128)}, f32[512,512]{1,0:T(8,128)}), (f32[64,512]{0,1:T(8,128)}, f32[512,512]{1,0:T(8,128)})) %all-reduce.3.cloned.1.call-update) | async-done | bytes 1179664 | tf_op jit(solution)/shard_map/psum | solution.py:190
  289.1 1.7 copy.9
  291.5 2.2 fusion.23
  293.7 14.2 %convolution_subtract_fusion = f32[512,4096]{1,0:T(8,128)} fusion(f32[512,4096]{1,0:T(8,128)} %param.5, f32[512,512]{1,0:T(8,128)S(1)} %fusion.23, f32[4096,512]{1,0:T(8,128)} %vr_ref.7), kind=kOutput, calls=%fused_computation | convolution fusion | flops 6444548096 | bytes 26214400 | tf_op jit(solution)/shard_map/dot_general | solution.py:112
  307.9 10.7 %collective-permute-done.14 = f32[512,512]{1,0:T(8,128)} collective-permute-done((f32[512,512]{1,0:T(8,128)}, f32[512,512]{1,0:T(8,128)}, u32[]{:S(2)}, u32[]{:S(2)}) %collective-permute-start.14) | collective-permute-done | bytes 1048608 | tf_op jit(solution)/shard_map/ppermute | solution.py:193
  318.7 2.2 fusion.18
  320.9 1.0 fusion.19
  322.0 2.0 fusion.20
  324.0 3.2 fusion.21
  327.2 1.0 fusion.22
  328.2 2.0 convolution_subtract_fusion.1.zc_ref
  330.2 21.4 %update_chunk.4.rest_0_ = f32[4096,2048]{1,0:T(8,128)} custom-call(s32[9]{0:T(128)} %get-tuple-element.32.order_ref, f32[4096,2048]{1,0:T(8,128)} %a_ref.15, f32[2048,512]{1,0:T(8,128)} %fusion.4.near_ref, f32[2048,512]{1,0:T(8,128)} %collective-permute-done.12.far_ref, f32[4096,512]{1,0:T(8,128)} %vr_ref.7, f32[512,512]{1,0:T(8,128)} %copy-done.3, ...), custom_call_target="tpu_custom_call" | custom-call | flops 12884901888 | bytes 33554432 | tf_op jit(solution)/shard_map/update_chunk/pallas_call | solution.py:91
  351.6 2.4 sub.47.zc_ref
  354.1 21.3 %update_chunk.5.rest_0_ = f32[4096,2048]{1,0:T(8,128)} custom-call(s32[9]{0:T(128)} %get-tuple-element.34.order_ref, f32[4096,2048]{1,0:T(8,128)} %a_ref.15, f32[2048,512]{1,0:T(8,128)} %fusion.4.near_ref, f32[2048,512]{1,0:T(8,128)} %collective-permute-done.12.far_ref, f32[4096,512]{1,0:T(8,128)} %vr_ref.7, ...), custom_call_target="tpu_custom_call", output_to_operand_aliasing={{}: (7, {})} | custom-call | flops 12884901888 | bytes 33554432 | tf_op jit(solution)/shard_map/update_chunk/pallas_call | solution.py:91
  375.3 2.4 sub.48.zc_ref
  377.8 21.1 %update_chunk.6.rest_0_ = f32[4096,2048]{1,0:T(8,128)} custom-call(s32[9]{0:T(128)} %get-tuple-element.33.order_ref, f32[4096,2048]{1,0:T(8,128)} %a_ref.15, f32[2048,512]{1,0:T(8,128)} %fusion.4.near_ref, f32[2048,512]{1,0:T(8,128)} %collective-permute-done.12.far_ref, f32[4096,512]{1,0:T(8,128)} %vr_ref.7, ...), custom_call_target="tpu_custom_call", output_to_operand_aliasing={{}: (7, {})} | custom-call | flops 12884901888 | bytes 33554432 | tf_op jit(solution)/shard_map/update_chunk/pallas_call | solution.py:91
  398.9 2.4 sub.49.zc_ref
  401.3 21.2 %update_chunk.7 = f32[4096,2048]{1,0:T(8,128)} custom-call(s32[9]{0:T(128)} %get-tuple-element.35.order_ref, f32[4096,2048]{1,0:T(8,128)} %a_ref.15, f32[2048,512]{1,0:T(8,128)} %fusion.4.near_ref, f32[2048,512]{1,0:T(8,128)} %collective-permute-done.12.far_ref, f32[4096,512]{1,0:T(8,128)} %vr_ref.7, ...), custom_call_target="tpu_custom_call", output_to_operand_aliasing={{}: (7, {})} | custom-call | flops 12884901888 | bytes 33554432 | tf_op jit(solution)/shard_map/update_chunk/pallas_call | solution.py:91
  (54 shorter events, 4.2 us)
Async XLA Ops:
  7.2 184.1 %copy-start = (f32[512,512]{1,0:T(8,128)S(1)}, f32[512,512]{1,0:T(8,128)}, u32[]{:S(2)}) copy-start(f32[512,512]{1,0:T(8,128)} %param.7) | copy-start | bytes 3145732
  7.2 179.9 %reduce-scatter.4.cloned.1.call-start = ((), (), s32[]{:S(2)}) async-start(), calls=%async_computation.2 | async-start | bytes 1179648
  8.6 28.3 %copy-start.3 = (f32[512,512]{1,0:T(8,128)}, f32[512,512]{1,0:T(8,128)S(1)}, u32[]{:S(2)}) copy-start(f32[512,512]{1,0:T(8,128)S(1)} %constant_dynamic-slice_fusion.v_ref.vc_ref) | copy-start | bytes 3145732
  8.6 28.3 %collective-permute-start = (f32[512,512]{1,0:T(8,128)S(1)}, f32[512,512]{1,0:T(8,128)S(1)}, u32[]{:S(2)}, u32[]{:S(2)}) collective-permute-start(f32[512,512]{1,0:T(8,128)S(1)} %constant_dynamic-slice_fusion.v_ref.vc_ref), channel_id=1, source_target_pairs={{0,8},{8,16},{16,24},{24,0},{1,9},{9,17},{17,25},{25,1},{2,10},{10... | collective-permute-start | bytes 3145736 | tf_op jit(solution)/shard_map/ppermute | solution.py:178
  36.9 12.9 %copy-start.5 = (f32[512,512]{1,0:T(8,128)}, f32[512,512]{1,0:T(8,128)S(1)}, u32[]{:S(2)}) copy-start(f32[512,512]{1,0:T(8,128)S(1)} %collective-permute-done.v_ref.vc_ref) | copy-start | bytes 3145732
  36.9 26.2 %collective-permute-start.1 = (f32[512,512]{1,0:T(8,128)S(1)}, f32[512,512]{1,0:T(8,128)}, u32[]{:S(2)}, u32[]{:S(2)}) collective-permute-start(f32[512,512]{1,0:T(8,128)S(1)} %collective-permute-done.v_ref.vc_ref), channel_id=1, source_target_pairs={{0,8},{8,16},{16,24},{24,0},{1,9},{9,17},{17,25},{25,1},{2,10},{10... | collective-permute-start | bytes 3145736 | tf_op jit(solution)/shard_map/ppermute | solution.py:178
  63.1 28.6 %collective-permute-start.2 = (f32[512,512]{1,0:T(8,128)}, f32[512,512]{1,0:T(8,128)S(1)}, u32[]{:S(2)}, u32[]{:S(2)}) collective-permute-start(f32[512,512]{1,0:T(8,128)} %collective-permute-done.1.v_ref.vc_ref), channel_id=1, source_target_pairs={{0,8},{8,16},{16,24},{24,0},{1,9},{9,17},{17,25},{25,1},{2,10},{10... | collective-permute-start | bytes 3145736 | tf_op jit(solution)/shard_map/ppermute | solution.py:178
  91.8 1.0 copy-start.7
  106.9 19.2 %copy-start.2 = (f32[4096,512]{1,0:T(8,128)S(1)}, f32[4096,512]{1,0:T(8,128)}, u32[]{:S(2)}) copy-start(f32[4096,512]{1,0:T(8,128)} %apply_chunk.7) | copy-start | bytes 25165828
  128.5 7.5 %collective-permute-start.3 = (f32[2,2,512,512]{3,2,1,0:T(8,128)}, f32[2,2,512,512]{3,2,1,0:T(8,128)}, u32[]{:S(2)}, u32[]{:S(2)}) collective-permute-start(f32[2,2,512,512]{3,2,1,0:T(8,128)} %dynamic-slice_bitcast_fusion), channel_id=1, source_target_pairs={{0,2},{2,0},{4,6},{6,4},{1,3},{3,1},{5,7},{7,5},{8,10},{10,8},{12,... | collective-permute-start | bytes 12582920 | tf_op jit(solution)/shard_map/ppermute | solution.py:117
  140.9 1.3 copy-start.9
  143.3 25.5 %collective-permute-start.6 = (f32[2,256,512]{2,1,0:T(8,128)}, f32[2,256,512]{2,1,0:T(8,128)}, u32[]{:S(2)}, u32[]{:S(2)}) collective-permute-start(f32[2,256,512]{2,1,0:T(8,128)} %dynamic-slice_bitcast_fusion.1), channel_id=1, source_target_pairs={{0,1},{1,0},{2,3},{3,2},{4,5},{5,4},{6,7},{7,6},{8,9},{9,8},{10,11... | collective-permute-start | bytes 3145736 | tf_op jit(solution)/shard_map/ppermute | solution.py:117
  145.8 27.3 %collective-permute-start.4 = (f32[2,256,512]{2,1,0:T(8,128)}, f32[2,256,512]{2,1,0:T(8,128)}, u32[]{:S(2)}, u32[]{:S(2)}) collective-permute-start(f32[2,256,512]{2,1,0:T(8,128)} %dynamic-slice_bitcast_fusion.2), channel_id=1, source_target_pairs={{0,4},{2,6},{4,0},{6,2},{1,5},{3,7},{5,1},{7,3},{8,12},{10,14},{12... | collective-permute-start | bytes 3145736 | tf_op jit(solution)/shard_map/ppermute | solution.py:117
  149.9 139.2 %all-reduce.3.cloned.1.call-start = ((), (), s32[]{:S(2)}) async-start(), calls=%async_computation.3 | async-start | bytes 2621440 | tf_op jit(solution)/shard_map/psum | solution.py:190
  170.7 3.9 copy-start.12
  171.6 17.2 %collective-permute-start.7 = (f32[256,512]{1,0:T(8,128)}, f32[256,512]{1,0:T(8,128)}, u32[]{:S(2)}, u32[]{:S(2)}) collective-permute-start(f32[256,512]{1,0:T(8,128)} %dynamic-slice_bitcast_fusion.3), channel_id=1, source_target_pairs={{0,4},{2,6},{4,0},{6,2},{1,5},{3,7},{5,1},{7,3},{8,12},{10,14},{12... | collective-permute-start | bytes 1572872 | tf_op jit(solution)/shard_map/ppermute | solution.py:117
  174.6 1.0 copy-start.13
  175.6 14.5 %collective-permute-start.5 = (f32[256,512]{1,0:T(8,128)S(1)}, f32[256,512]{1,0:T(8,128)S(1)}, u32[]{:S(2)}, u32[]{:S(2)}) collective-permute-start(f32[256,512]{1,0:T(8,128)S(1)} %dynamic-slice_bitcast_fusion.4), channel_id=1, source_target_pairs={{0,1},{1,0},{2,3},{3,2},{4,5},{5,4},{6,7},{7,6},{8,9},{9,8},{10,11... | collective-permute-start | bytes 1572872 | tf_op jit(solution)/shard_map/ppermute | solution.py:117
  192.4 13.8 %collective-permute-start.9 = (f32[1,256,512]{2,1,0:T(8,128)S(1)}, f32[1,256,512]{2,1,0:T(8,128)S(1)}, u32[]{:S(2)}, u32[]{:S(2)}) collective-permute-start(f32[1,256,512]{2,1,0:T(8,128)S(1)} %get-tuple-element.30), channel_id=1, source_target_pairs={{0,4},{2,6},{4,0},{6,2},{1,5},{3,7},{5,1},{7,3},{8,12},{10,14},{12... | collective-permute-start | bytes 1572872 | tf_op jit(solution)/shard_map/ppermute | solution.py:117
  193.9 14.6 %collective-permute-start.8 = (f32[1,256,512]{2,1,0:T(8,128)S(1)}, f32[1,256,512]{2,1,0:T(8,128)S(1)}, u32[]{:S(2)}, u32[]{:S(2)}) collective-permute-start(f32[1,256,512]{2,1,0:T(8,128)S(1)} %get-tuple-element.31), channel_id=1, source_target_pairs={{0,1},{1,0},{2,3},{3,2},{4,5},{5,4},{6,7},{7,6},{8,9},{9,8},{10,11... | collective-permute-start | bytes 1572872 | tf_op jit(solution)/shard_map/ppermute | solution.py:117
  207.2 24.4 %collective-permute-start.10 = (f32[2,256,512]{2,1,0:T(8,128)}, f32[2,256,512]{2,1,0:T(8,128)}, u32[]{:S(2)}, u32[]{:S(2)}) collective-permute-start(f32[2,256,512]{2,1,0:T(8,128)} %pad_maximum_fusion), channel_id=1, source_target_pairs={{0,1},{1,0},{2,3},{3,2},{4,5},{5,4},{6,7},{7,6},{8,9},{9,8},{10,11... | collective-permute-start | bytes 3145736 | tf_op jit(solution)/shard_map/ppermute | solution.py:117
  209.6 24.1 %collective-permute-start.11 = (f32[2,256,512]{2,1,0:T(8,128)}, f32[2,256,512]{2,1,0:T(8,128)}, u32[]{:S(2)}, u32[]{:S(2)}) collective-permute-start(f32[2,256,512]{2,1,0:T(8,128)} %pad_maximum_fusion.1), channel_id=1, source_target_pairs={{0,4},{2,6},{4,0},{6,2},{1,5},{3,7},{5,1},{7,3},{8,12},{10,14},{12... | collective-permute-start | bytes 3145736 | tf_op jit(solution)/shard_map/ppermute | solution.py:117
  210.2 108.4 %all-gather.2.cloned.1.call-start = ((), (), s32[]{:S(2)}) async-start(), calls=%async_computation.1 | async-start | bytes 1179648 | tf_op jit(solution)/shard_map/all_gather | solution.py:190
  240.3 90.0 %collective-permute-start.12 = (f32[2048,512]{1,0:T(8,128)}, f32[2048,512]{1,0:T(8,128)}, u32[]{:S(2)}, u32[]{:S(2)}) collective-permute-start(f32[2048,512]{1,0:T(8,128)} %fusion.4.near_ref), channel_id=1, source_target_pairs={{0,2},{2,0},{4,6},{6,4},{1,3},{3,1},{5,7},{7,5},{8,10},{10,8},{12,... | collective-permute-start | bytes 12582920 | tf_op jit(solution)/shard_map/ppermute | solution.py:117
  240.3 51.2 %collective-permute-start.13 = (f32[512,512]{1,0:T(8,128)S(1)}, f32[512,512]{1,0:T(8,128)}, u32[]{:S(2)}, u32[]{:S(2)}) collective-permute-start(f32[512,512]{1,0:T(8,128)S(1)} %fusion), channel_id=1, source_target_pairs={{0,8},{8,16},{16,24},{24,0},{1,9},{9,17},{17,25},{25,1},{2,10},{10... | collective-permute-start | bytes 3145736 | tf_op jit(solution)/shard_map/ppermute | solution.py:193
  291.5 27.2 %collective-permute-start.14 = (f32[512,512]{1,0:T(8,128)}, f32[512,512]{1,0:T(8,128)}, u32[]{:S(2)}, u32[]{:S(2)}) collective-permute-start(f32[512,512]{1,0:T(8,128)} %collective-permute-done.13), channel_id=1, source_target_pairs={{0,8},{8,16},{16,24},{24,0},{1,9},{9,17},{17,25},{25,1},{2,10},{10... | collective-permute-start | bytes 3145736 | tf_op jit(solution)/shard_map/ppermute | solution.py:193
  307.9 14.0 %copy-start.6 = (f32[512,512]{1,0:T(8,128)S(1)}, f32[512,512]{1,0:T(8,128)}, u32[]{:S(2)}) copy-start(f32[512,512]{1,0:T(8,128)} %copy-done.5) | copy-start | bytes 3145732
  318.7 80.2 %collective-permute-start.15 = (f32[512,512]{1,0:T(8,128)}, f32[512,512]{1,0:T(8,128)}, u32[]{:S(2)}, u32[]{:S(2)}) collective-permute-start(f32[512,512]{1,0:T(8,128)} %collective-permute-done.14), channel_id=1, source_target_pairs={{0,8},{8,16},{16,24},{24,0},{1,9},{9,17},{17,25},{25,1},{2,10},{10... | collective-permute-start | bytes 3145736 | tf_op jit(solution)/shard_map/ppermute | solution.py:193
  320.9 6.2 %copy-start.8 = (f32[512,512]{1,0:T(8,128)S(1)}, f32[512,512]{1,0:T(8,128)}, u32[]{:S(2)}) copy-start(f32[512,512]{1,0:T(8,128)} %copy-done.7) | copy-start | bytes 3145732
  322.0 6.2 %copy-start.4 = (f32[512,512]{1,0:T(8,128)S(1)}, f32[512,512]{1,0:T(8,128)}, u32[]{:S(2)}) copy-start(f32[512,512]{1,0:T(8,128)} %copy-done.3) | copy-start | bytes 3145732
  330.2 21.4 %copy-start.11 = (f32[512,512]{1,0:T(8,128)S(1)}, f32[512,512]{1,0:T(8,128)}, u32[]{:S(2)}) copy-start(f32[512,512]{1,0:T(8,128)} %fusion.20) | copy-start | bytes 3145732
  354.1 21.3 %copy-start.10 = (f32[512,512]{1,0:T(8,128)S(1)}, f32[512,512]{1,0:T(8,128)}, u32[]{:S(2)}) copy-start(f32[512,512]{1,0:T(8,128)} %fusion.21) | copy-start | bytes 3145732
  401.3 21.2 %copy-start.1 = (f32[512,512]{1,0:T(8,128)S(1)}, f32[512,512]{1,0:T(8,128)}, u32[]{:S(2)}) copy-start(f32[512,512]{1,0:T(8,128)} %param.7) | copy-start | bytes 3145732
Sparse Core Ops, SparseCore 0:
  150.0 37.0 reduce-scatter.3
  210.4 78.6 all-reduce.2
  291.5 20.6 all-gather.1
